TPU v7x, 32 devices: a whole 2x2x4 slice. The times are simulated.
32 devices in a mesh: sub: 8 (over z, y), sec: 4 (over x, core).
Axes of the slice: x: 2, y: 2, z: 4, core: 2. Of those that a mesh axis runs over, the one named last changes fastest.
Arguments:
- start_vectors: bfloat16 [32, 3, 256, 512], P(None, None, 'sub', 'sec'), may hold values from -6 to 6
- stiffness: bfloat16 [3, 256, 512], P(None, 'sub', 'sec'), may hold values from 1.5 to 15
- coupling: bfloat16 [256, 512], P('sub', 'sec'), may hold values from -0.5 to 0.5
- kept_ranks: int32 [8, 4], P('sub', 'sec'), may hold values from 16 to 32, as said below
- level_start: float32 [256, 16], P('sub'), may hold values from -6 to 6
Outputs:
- prolonged: float32 [16, 3, 256, 512], P(None, None, 'sub', 'sec')
Inputs may be any that keep to these rules, and one draw needn't show every extreme that they name: `kept_ranks`: every subdomain keeps at least half of its 32 vectors; some subdomain keeps all 32 and some keeps exactly half.
All inputs are finite; a program needn't handle non-finite values.
Results may differ from a plain program's by a relative error of at most 0.0003.
Values may be sent and summed in bfloat16 or wider, within the bound.
No kernel may reach another device: no remote copies, remote signals or barrier semaphores. Data moves between devices by JAX's collectives and lax.ppermute only.
A program may use at most 64 MiB of HBM per device.

v0:
```python
import math
import jax
import jax.numpy as jnp
from jax import lax
from jax.sharding import PartitionSpec as P

CX = 32
H = 4
CY = 128
NV = 32
ITERS = 2
LEVEL_ITERS = 2
XEXT = 40
YEXT = 136
highest = lax.Precision.HIGHEST


def with_halo(x, sides, width):
    for axis, dim in sides:
        devices, length = (lax.axis_size(axis), x.shape[dim])
        up = [(i, (i + 1) % devices) for i in range(devices - 1)]
        down = [(j, i) for i, j in up]
        last = lax.slice_in_dim(x, length - width, length, axis=dim)
        leading = lax.slice_in_dim(x, 0, width, axis=dim)
        before = lax.ppermute(last, axis, up)
        after = lax.ppermute(leading, axis, down)
        x = jnp.concatenate([before, x, after], axis=dim)
    return x


def from_behind(block, axis, distance):
    devices = range(lax.axis_size(axis))
    route = [(i - distance, i) for i in devices if i - distance in devices]
    return lax.ppermute(block, axis, route)


def apply_operator(vectors, stiff_diag, shear_term, inside):
    padded = jnp.pad(vectors, ((0, 0), (0, 0), (1, 1), (1, 1)))
    beside = (
        padded[:, :, 2:, 1:-1]
        + padded[:, :, :-2, 1:-1]
        + padded[:, :, 1:-1, 2:]
        + padded[:, :, 1:-1, :-2]
    )
    others = jnp.sum(vectors, axis=1, keepdims=True) - vectors
    return ((4.0 + stiff_diag) * vectors - beside + shear_term * others) * inside


def orthonormal(work):
    shape_before = work.shape
    flat = work.reshape(shape_before[0], -1)
    gram = jnp.dot(flat, flat.T, precision=highest)
    lower = jnp.linalg.cholesky(gram)
    solved = lax.linalg.triangular_solve(lower, flat, left_side=True, lower=True)
    return solved.reshape(shape_before)


def subspace_basis(vectors, stiff_diag, shear_term, inside, rank):
    for iteration in range(ITERS):
        vectors = orthonormal(apply_operator(vectors, stiff_diag, shear_term, inside))
    live = (jnp.arange(NV, dtype=jnp.int32) < rank).astype(jnp.float32)
    basis = vectors * live[:, None, None, None]
    image = apply_operator(basis, stiff_diag, shear_term, inside)
    self_block = jnp.dot(basis.reshape(NV, -1), image.reshape(NV, -1).T, precision=highest)
    return (basis, self_block)


def on_device(start_vectors, stiffness, coupling, kept_ranks, level_start):
    span_count = lax.axis_size("sub")
    sect_count = lax.axis_size("sec")
    stacked = jnp.concatenate(
        [start_vectors.reshape(NV * 3, CX, CY), stiffness, coupling[None]], axis=0
    )
    extended = with_halo(stacked, (("sub", 1), ("sec", 2)), H)
    vectors = extended[: NV * 3].astype(jnp.float32).reshape(NV, 3, XEXT, YEXT)
    stiff_diag = extended[NV * 3 : NV * 3 + 3].astype(jnp.float32)
    shear_term = extended[NV * 3 + 3].astype(jnp.float32)
    row_global = lax.axis_index("sub") * CX - H + lax.iota(jnp.int32, XEXT)
    col_global = lax.axis_index("sec") * CY - H + lax.iota(jnp.int32, YEXT)
    row_inside = (row_global >= 0) & (row_global < span_count * CX)
    col_inside = (col_global >= 0) & (col_global < sect_count * CY)
    inside = (row_inside[:, None] & col_inside[None, :]).astype(jnp.float32)
    basis, self_block = subspace_basis(vectors, stiff_diag, shear_term, inside, kept_ranks[0, 0])
    lower_next = from_behind(basis[:, :, : 2 * H, :], "sub", -1)
    upper_rim = (4.0 + stiff_diag[:, CX:, :]) * basis[:, :, CX:, :]
    couple_block = jnp.einsum("acxy,bcxy->ab", upper_rim, lower_next, precision=highest)
    own_rows = level_start
    couple_prev = from_behind(couple_block, "sub", 1)
    for iteration in range(LEVEL_ITERS):
        rows_next = from_behind(own_rows, "sub", -1)
        image = jnp.dot(self_block, own_rows, precision=highest)
        image = image + jnp.dot(couple_block, rows_next, precision=highest)
        rows_prev = from_behind(own_rows, "sub", 1)
        image = image + jnp.dot(couple_prev.T, rows_prev, precision=highest)
        gram = lax.psum(jnp.dot(image.T, image, precision=highest), "sub")
        lower = jnp.linalg.cholesky(gram)
        own_rows = lax.linalg.triangular_solve(lower, image.T, left_side=True, lower=True).T
    factor = math.sqrt(span_count * 3 * XEXT * YEXT)
    owned = basis[:, :, H : H + CX, H : H + CY]
    return factor * jnp.einsum("ak,acxy->kcxy", own_rows, owned, precision=highest)


def solution(mesh):
    placed = (
        P(None, None, "sub", "sec"),
        P(None, "sub", "sec"),
        P("sub", "sec"),
        P("sub", "sec"),
        P("sub", None),
    )
    return jax.shard_map(
        on_device,
        mesh=mesh,
        in_specs=placed,
        out_specs=P(None, None, "sub", "sec"),
        check_vma=False,
    )
```

profile of v0, /device:TPU:0, one launch (start us, length us, event | category | flops | bytes accessed | tf_op | source)
XLA Modules:
  0.0 206.8 jit_solution(7046180540235981564)
XLA Ops:
  0.0 4.9 %collective-permute-start.7 = (f32[32,16]{0,1:T(8,128)}, f32[32,16]{0,1:T(8,128)S(1)}, u32[]{:S(2)}, u32[]{:S(2)}) collective-permute-start(f32[32,16]{0,1:T(8,128)} %param.15), channel_id=1, source_target_pairs={{0,4},{4,8},{8,12},{12,16},{16,20},{20,24},{24,28},{1,5},{5,9},{9,... | collective-permute-start | bytes 6152 | tf_op jit(solution)/shard_map/ppermute | solution.py:34
  4.9 1.3 collective-permute-start.5
  6.2 1.2 pad_maximum_fusion.4
  7.4 4.6 %collective-permute-start = (bf16[100,4,128]{2,1,0:T(4,128)(2,1)S(1)}, bf16[100,4,128]{2,1,0:T(4,128)(2,1)S(1)}, u32[]{:S(2)}, u32[]{:S(2)}) collective-permute-start(bf16[100,4,128]{2,1,0:T(4,128)(2,1)S(1)} %get-tuple-element.15), channel_id=1, source_target_pairs={{0,4},{4,8},{8,12},{12,16},{16,20},{20,24},{24,28},{1,5},{5,9},{9,... | collective-permute-start | bytes 307208 | tf_op jit(solution)/shard_map/ppermute | solution.py:25
  11.9 1.3 collective-permute-start.1
  14.2 4.7 %collective-permute-done.1 = bf16[100,4,128]{2,1,0:T(4,128)(2,1)S(1)} collective-permute-done((bf16[100,4,128]{2,1,0:T(4,128)(2,1)S(1)}, bf16[100,4,128]{2,1,0:T(4,128)(2,1)S(1)}, u32[]{:S(2)}, u32[]{:S(2)}) %collective-permute-start.1) | collective-permute-done | bytes 102432 | tf_op jit(solution)/shard_map/ppermute | solution.py:26
  18.9 1.7 pad_maximum_fusion.1
  21.0 0.7 copy.33
  22.4 1.3 collective-permute-start.3
  23.7 3.0 %collective-permute-start.2 = (bf16[100,40,4]{0,1,2:T(8,128)(2,1)S(1)}, bf16[100,40,4]{0,1,2:T(8,128)(2,1)S(1)}, u32[]{:S(2)}, u32[]{:S(2)}) collective-permute-start(bf16[100,40,4]{0,1,2:T(8,128)(2,1)S(1)} %copy.33), channel_id=1, source_target_pairs={{0,1},{1,2},{2,3},{4,5},{5,6},{6,7},{8,9},{9,10},{10,11},{12,13},{... | collective-permute-start | bytes 96008 | tf_op jit(solution)/shard_map/ppermute | solution.py:25
  26.7 0.8 collective-permute-done.2
  28.9 4.9 %pad_maximum_fusion = bf16[100,40,136]{2,1,0:T(8,128)(2,1)S(1)} fusion(bf16[100,40,4]{2,1,0:T(8,128)(2,1)S(1)} %copy.36, bf16[100,4,128]{2,1,0:T(4,128)(2,1)S(1)} %collective-permute-done.1, bf16[1,32,128]{2,1,0:T(8,128)(2,1)S(1)} %bitcast.112, bf16[3,32,128]{2,1,0:T(8,128)(2,1)S(1)} %copy-done.2, bf16[96,32,128]{2,1,0:T(8,128)(2,1)S(1)} %bitcast.105, ...), kind=kLoop, calls=%fused_computation.24 | loop fusion | flops 7616000 | bytes 2176000 | tf_op jit(solution)/shard_map/concatenate | solution.py:27
  35.4 3.0 %add_multiply_fusion.1 = f32[32,3,40,136]{3,0,2,1:T(8,128)S(1)} fusion(f32[32,3,40,136]{3,0,2,1:T(8,128)S(1)} %copy.37, f32[40,136]{1,0:T(8,128)S(1)} %and_convert_fusion, f32[32,40,136]{2,0,1:T(8,128)S(1)} %copy.39, f32[40,136]{1,0:T(8,128)S(1)} %fusion.29, f32[3,40,136]{2,1,0:T(8,128)S(1)} %get-tuple-element.10), kind=kLoop, calls=%fused_computation.20 | loop fusion | flops 4700160 | bytes 4983040 | tf_op jit(solution)/shard_map/mul | solution.py:46
  38.4 3.2 %convolution_bitcast_fusion.2 = f32[32,32]{1,0:T(8,128)S(1)} fusion(f32[32,3,40,136]{3,0,2,1:T(8,128)S(1)} %add_multiply_fusion.1), kind=kOutput, calls=%fused_computation.35 | convolution fusion | flops 200540160 | bytes 2093056 | tf_op jit(solution)/shard_map/dot_general | solution.py:52
  41.6 4.2 %copy.42 = f32[32,3,40,136]{3,2,1,0:T(8,128)} copy(f32[32,3,40,136]{3,0,2,1:T(8,128)S(1)} %add_multiply_fusion.1) | data formatting | bytes 4177920 | tf_op jit(solution)/shard_map/mul | solution.py:46
  45.8 3.6 %reshape.107 = f32[32,16320]{1,0:T(8,128)S(1)} reshape(f32[32,3,40,136]{3,2,1,0:T(8,128)} %copy.42) | data formatting | bytes 4177920 | tf_op jit(solution)/shard_map/reshape | solution.py:51
  49.5 2.9 %cholesky.86 = f32[32,32]{1,0:T(8,128)S(1)} custom-call(f32[32,32]{1,0:T(8,128)S(1)} %fusion.37), custom_call_target="Cholesky" | custom-call | tf_op jit(solution)/shard_map/jit(cholesky)/cholesky | solution.py:53
  53.7 2.4 %custom-call.12 = f32[1,32,32]{1,2,0:T(8,128)S(1)} custom-call(f32[1,32,32]{2,1,0:T(8,128)S(1)} %fusion.30), custom_call_target="InvertDiagBlocksLowerTriangular" | custom-call | tf_op jit(solution)/shard_map/triangular_solve/custom-call.2 | solution.py:54
  56.2 3.3 %fusion.35 = f32[32,16320]{1,0:T(8,128)} fusion(f32[32,16320]{1,0:T(8,128)S(1)} %reshape.107, f32[1,32,32]{1,2,0:T(8,128)S(1)} %custom-call.12), kind=kOutput, calls=%fused_computation.62 | convolution fusion | flops 200540160 | bytes 4182016 | tf_op jit(solution)/shard_map/triangular_solve/dot.1 | solution.py:54
  59.4 5.0 %reshape.108 = f32[32,3,40,136]{3,2,1,0:T(8,128)} reshape(f32[32,16320]{1,0:T(8,128)} %fusion.35) | data formatting | bytes 4177920 | tf_op jit(solution)/shard_map/reshape | solution.py:55
  64.5 5.2 %copy.43 = f32[32,3,40,136]{3,0,2,1:T(8,128)} copy(f32[32,3,40,136]{3,2,1,0:T(8,128)} %reshape.108) | data formatting | bytes 4177920 | tf_op jit(solution)/shard_map/reshape | solution.py:55
  69.7 2.6 %reduce_sum.28 = f32[32,40,136]{2,1,0:T(8,128)S(1)} reduce(f32[32,3,40,136]{3,2,1,0:T(8,128)} %reshape.108, f32[]{:T(128)} %constant.80.clone.1), dimensions={1}, to_apply=%region_3.0 | reduce | flops 348160 | bytes 2785284 | tf_op jit(solution)/shard_map/reduce_sum | solution.py:45
  72.7 9.0 %add_multiply_fusion = f32[32,3,40,136]{3,0,2,1:T(8,128)S(1)} fusion(f32[32,3,40,136]{3,0,2,1:T(8,128)} %copy.43, f32[32,40,136]{2,0,1:T(8,128)S(1)} %copy.45, f32[40,136]{1,0:T(8,128)S(1)} %and_convert_fusion, f32[40,136]{1,0:T(8,128)S(1)} %fusion.29, f32[3,40,136]{2,1,0:T(8,128)S(1)} %get-tuple-element.10), kind=kLoop, calls=%fused_computation.16 | loop fusion | flops 4700160 | bytes 4983040 | tf_op jit(solution)/shard_map/mul | solution.py:46
  81.7 3.2 %convolution_bitcast_fusion.1 = f32[32,32]{1,0:T(8,128)S(1)} fusion(f32[32,3,40,136]{3,0,2,1:T(8,128)S(1)} %add_multiply_fusion), kind=kOutput, calls=%fused_computation.34 | convolution fusion | flops 200540160 | bytes 2093056 | tf_op jit(solution)/shard_map/dot_general | solution.py:52
  84.9 4.2 %copy.48 = f32[32,3,40,136]{3,2,1,0:T(8,128)} copy(f32[32,3,40,136]{3,0,2,1:T(8,128)S(1)} %add_multiply_fusion) | data formatting | bytes 4177920 | tf_op jit(solution)/shard_map/mul | solution.py:46
  89.0 3.1 %reshape.109 = f32[32,16320]{1,0:T(8,128)S(1)} reshape(f32[32,3,40,136]{3,2,1,0:T(8,128)} %copy.48) | data formatting | bytes 4177920 | tf_op jit(solution)/shard_map/reshape | solution.py:51
  92.2 2.9 %cholesky.97 = f32[32,32]{1,0:T(8,128)S(1)} custom-call(f32[32,32]{1,0:T(8,128)S(1)} %fusion.34), custom_call_target="Cholesky" | custom-call | tf_op jit(solution)/shard_map/jit(cholesky)/cholesky | solution.py:53
  96.5 2.4 %custom-call.13 = f32[1,32,32]{1,2,0:T(8,128)S(1)} custom-call(f32[1,32,32]{2,1,0:T(8,128)S(1)} %fusion.31), custom_call_target="InvertDiagBlocksLowerTriangular" | custom-call | tf_op jit(solution)/shard_map/triangular_solve/custom-call.2 | solution.py:54
  98.9 3.3 %fusion.32 = f32[32,16320]{1,0:T(8,128)} fusion(f32[32,16320]{1,0:T(8,128)S(1)} %reshape.109, f32[1,32,32]{1,2,0:T(8,128)S(1)} %custom-call.13), kind=kOutput, calls=%fused_computation.58 | convolution fusion | flops 200540160 | bytes 4182016 | tf_op jit(solution)/shard_map/triangular_solve/dot.1 | solution.py:54
  102.2 5.2 %reshape.110 = f32[32,3,40,136]{3,2,1,0:T(8,128)} reshape(f32[32,16320]{1,0:T(8,128)} %fusion.32) | data formatting | bytes 4177920 | tf_op jit(solution)/shard_map/reshape | solution.py:55
  107.4 3.9 %fusion.52 = (f32[32,40,136]{2,0,1:T(8,128)S(1)}, f32[32,3,40,136]{3,0,2,1:T(8,128)S(1)}) fusion(f32[32]{0:T(128)S(1)} %compare_convert_fusion, f32[32,3,40,136]{3,2,1,0:T(8,128)} %reshape.110), kind=kLoop, calls=%fused_computation.97 | loop fusion | flops 870400 | bytes 4874368 | tf_op jit(solution)/shard_map/reduce_sum | solution.py:45
  111.4 5.0 %fusion.25 = f32[32,32]{1,0:T(8,128)S(1)} fusion(f32[32,3,40,136]{3,0,2,1:T(8,128)S(1)} %get-tuple-element.8, f32[32,40,136]{2,0,1:T(8,128)S(1)} %get-tuple-element.6, f32[40,136]{1,0:T(8,128)S(1)} %and_convert_fusion, f32[40,136]{1,0:T(8,128)S(1)} %fusion.29, f32[3,40,136]{2,1,0:T(8,128)S(1)} %get-tuple-element.10), kind=kOutput, calls=%fused_computation.33 | convolution fusion | flops 205240320 | bytes 9383936 | tf_op jit(solution)/shard_map/dot_general | solution.py:64
  116.4 1.3 collective-permute-start.4
  117.9 21.1 %collective-permute-done.4 = f32[32,3,8,136]{3,0,2,1:T(8,128)S(1)} collective-permute-done((f32[32,3,8,136]{3,0,2,1:T(8,128)S(1)}, f32[32,3,8,136]{3,0,2,1:T(8,128)S(1)}, u32[]{:S(2)}, u32[]{:S(2)}) %collective-permute-start.4) | collective-permute-done | bytes 417824 | tf_op jit(solution)/shard_map/ppermute | solution.py:34
  139.0 0.8 convolution_bitcast_fusion
  139.8 5.1 %collective-permute-start.6 = (f32[32,32]{1,0:T(8,128)S(1)}, f32[32,32]{1,0:T(8,128)S(1)}, u32[]{:S(2)}, u32[]{:S(2)}) collective-permute-start(f32[32,32]{1,0:T(8,128)S(1)} %convolution_bitcast_fusion), channel_id=1, source_target_pairs={{0,4},{4,8},{8,12},{12,16},{16,20},{20,24},{24,28},{1,5},{5,9},{9,... | collective-permute-start | bytes 12296 | tf_op jit(solution)/shard_map/ppermute | solution.py:34
  145.0 1.3 collective-permute-done.6
  146.6 20.0 %psum.14 = f32[16,16]{0,1:T(8,128)S(1)} all-reduce(f32[16,16]{0,1:T(8,128)S(1)} %fusion.55), channel_id=1, replica_groups=mesh['sub'=8,'sec'=4] {'sub'}, use_global_device_ids=true, to_apply=%region_5.8 | all-reduce | flops 256 | bytes 2048 | tf_op jit(solution)/shard_map/psum | solution.py:95
  166.6 1.5 cholesky.108
  169.4 1.2 custom-call.14
  170.8 1.3 collective-permute-start.8
  172.3 4.6 %collective-permute-start.9 = (f32[32,16]{0,1:T(8,128)S(1)}, f32[32,16]{0,1:T(8,128)S(1)}, u32[]{:S(2)}, u32[]{:S(2)}) collective-permute-start(f32[32,16]{0,1:T(8,128)S(1)} %bitcast.116), channel_id=1, source_target_pairs={{0,4},{4,8},{8,12},{12,16},{16,20},{20,24},{24,28},{1,5},{5,9},{9,... | collective-permute-start | bytes 6152 | tf_op jit(solution)/shard_map/ppermute | solution.py:34
  177.0 1.2 collective-permute-done.9
  178.5 19.7 %psum.15 = f32[16,16]{0,1:T(8,128)S(1)} all-reduce(f32[16,16]{0,1:T(8,128)S(1)} %fusion.57), channel_id=1, replica_groups=mesh['sub'=8,'sec'=4] {'sub'}, use_global_device_ids=true, to_apply=%region_8.13 | all-reduce | flops 256 | bytes 2048 | tf_op jit(solution)/shard_map/psum | solution.py:95
  198.2 1.5 cholesky.119
  201.0 1.2 custom-call.15
  202.4 3.0 %fusion.22 = f32[16,3,32,128]{3,0,2,1:T(8,128)S(1)} fusion(f32[16,32,1,1]{1,0,3,2:T(8,128)S(1)} %convolution_bitcast_fusion.3, f32[32,3,40,136]{3,0,2,1:T(8,128)} %copy-done.1), kind=kOutput, calls=%fused_computation.31 | convolution fusion | flops 75694080 | bytes 2361344 | tf_op jit(solution)/shard_map/ak,acxy->kcxy/dot_general | solution.py:100
  205.5 1.1 copy.54
  (62 shorter events, 11.9 us)
Async XLA Ops:
  0.0 145.0 %collective-permute-start.7 = (f32[32,16]{0,1:T(8,128)}, f32[32,16]{0,1:T(8,128)S(1)}, u32[]{:S(2)}, u32[]{:S(2)}) collective-permute-start(f32[32,16]{0,1:T(8,128)} %param.15), channel_id=1, source_target_pairs={{0,4},{4,8},{8,12},{12,16},{16,20},{20,24},{24,28},{1,5},{5,9},{9,... | collective-permute-start | bytes 6152 | tf_op jit(solution)/shard_map/ppermute | solution.py:34
  4.9 140.0 %collective-permute-start.5 = (f32[32,16]{0,1:T(8,128)}, f32[32,16]{0,1:T(8,128)S(1)}, u32[]{:S(2)}, u32[]{:S(2)}) collective-permute-start(f32[32,16]{0,1:T(8,128)} %param.15), channel_id=1, source_target_pairs={{4,0},{8,4},{12,8},{16,12},{20,16},{24,20},{28,24},{5,1},{9,5},{13... | collective-permute-start | bytes 6152 | tf_op jit(solution)/shard_map/ppermute | solution.py:34
  7.4 6.8 %collective-permute-start = (bf16[100,4,128]{2,1,0:T(4,128)(2,1)S(1)}, bf16[100,4,128]{2,1,0:T(4,128)(2,1)S(1)}, u32[]{:S(2)}, u32[]{:S(2)}) collective-permute-start(bf16[100,4,128]{2,1,0:T(4,128)(2,1)S(1)} %get-tuple-element.15), channel_id=1, source_target_pairs={{0,4},{4,8},{8,12},{12,16},{16,20},{20,24},{24,28},{1,5},{5,9},{9,... | collective-permute-start | bytes 307208 | tf_op jit(solution)/shard_map/ppermute | solution.py:25
  11.9 7.0 %collective-permute-start.1 = (bf16[100,4,128]{2,1,0:T(4,128)(2,1)S(1)}, bf16[100,4,128]{2,1,0:T(4,128)(2,1)S(1)}, u32[]{:S(2)}, u32[]{:S(2)}) collective-permute-start(bf16[100,4,128]{2,1,0:T(4,128)(2,1)S(1)} %get-tuple-element.16), channel_id=1, source_target_pairs={{4,0},{8,4},{12,8},{16,12},{20,16},{24,20},{28,24},{5,1},{9,5},{13... | collective-permute-start | bytes 307208 | tf_op jit(solution)/shard_map/ppermute | solution.py:26
  20.6 8.2 %copy-start = (bf16[32,3,32,128]{3,2,1,0:T(8,128)(2,1)S(1)}, bf16[32,3,32,128]{3,2,1,0:T(8,128)(2,1)}, u32[]{:S(2)}) copy-start(bf16[32,3,32,128]{3,2,1,0:T(8,128)(2,1)} %param.11) | copy-start | bytes 2359300
  20.6 8.2 %copy-start.2 = (bf16[3,32,128]{2,1,0:T(8,128)(2,1)S(1)}, bf16[3,32,128]{2,1,0:T(8,128)(2,1)}, u32[]{:S(2)}) copy-start(bf16[3,32,128]{2,1,0:T(8,128)(2,1)} %param.12) | copy-start | bytes 73732
  20.6 8.2 %copy-start.3 = (bf16[32,128]{1,0:T(8,128)(2,1)S(1)}, bf16[32,128]{1,0:T(8,128)(2,1)}, u32[]{:S(2)}) copy-start(bf16[32,128]{1,0:T(8,128)(2,1)} %param.13) | copy-start | bytes 24580
  22.4 5.8 %collective-permute-start.3 = (bf16[100,40,4]{0,1,2:T(8,128)(2,1)S(1)}, bf16[100,40,4]{0,1,2:T(8,128)(2,1)S(1)}, u32[]{:S(2)}, u32[]{:S(2)}) collective-permute-start(bf16[100,40,4]{0,1,2:T(8,128)(2,1)S(1)} %copy.34), channel_id=1, source_target_pairs={{1,0},{2,1},{3,2},{5,4},{6,5},{7,6},{9,8},{10,9},{11,10},{13,12},{... | collective-permute-start | bytes 96008 | tf_op jit(solution)/shard_map/ppermute | solution.py:26
  23.7 3.9 %collective-permute-start.2 = (bf16[100,40,4]{0,1,2:T(8,128)(2,1)S(1)}, bf16[100,40,4]{0,1,2:T(8,128)(2,1)S(1)}, u32[]{:S(2)}, u32[]{:S(2)}) collective-permute-start(bf16[100,40,4]{0,1,2:T(8,128)(2,1)S(1)} %copy.33), channel_id=1, source_target_pairs={{0,1},{1,2},{2,3},{4,5},{5,6},{6,7},{8,9},{9,10},{10,11},{12,13},{... | collective-permute-start | bytes 96008 | tf_op jit(solution)/shard_map/ppermute | solution.py:25
  111.3 27.6 %copy-start.1 = (f32[32,3,40,136]{3,0,2,1:T(8,128)}, f32[32,3,40,136]{3,0,2,1:T(8,128)S(1)}, u32[]{:S(2)}) copy-start(f32[32,3,40,136]{3,0,2,1:T(8,128)S(1)} %get-tuple-element.8) | copy-start | bytes 6266884
  111.4 6.3 %copy-start.4 = (f32[32,16]{0,1:T(8,128)S(1)}, f32[32,16]{0,1:T(8,128)}, u32[]{:S(2)}) copy-start(f32[32,16]{0,1:T(8,128)} %param.15) | copy-start | bytes 6148
  116.4 22.6 %collective-permute-start.4 = (f32[32,3,8,136]{3,0,2,1:T(8,128)S(1)}, f32[32,3,8,136]{3,0,2,1:T(8,128)S(1)}, u32[]{:S(2)}, u32[]{:S(2)}) collective-permute-start(f32[32,3,8,136]{3,0,2,1:T(8,128)S(1)} %slice.109), channel_id=1, source_target_pairs={{4,0},{8,4},{12,8},{16,12},{20,16},{24,20},{28,24},{5,1},{9,5},{13... | collective-permute-start | bytes 1253384 | tf_op jit(solution)/shard_map/ppermute | solution.py:34
  139.8 6.5 %collective-permute-start.6 = (f32[32,32]{1,0:T(8,128)S(1)}, f32[32,32]{1,0:T(8,128)S(1)}, u32[]{:S(2)}, u32[]{:S(2)}) collective-permute-start(f32[32,32]{1,0:T(8,128)S(1)} %convolution_bitcast_fusion), channel_id=1, source_target_pairs={{0,4},{4,8},{8,12},{12,16},{16,20},{20,24},{24,28},{1,5},{5,9},{9,... | collective-permute-start | bytes 12296 | tf_op jit(solution)/shard_map/ppermute | solution.py:34
  170.8 6.0 %collective-permute-start.8 = (f32[32,16]{0,1:T(8,128)S(1)}, f32[32,16]{0,1:T(8,128)S(1)}, u32[]{:S(2)}, u32[]{:S(2)}) collective-permute-start(f32[32,16]{0,1:T(8,128)S(1)} %bitcast.115), channel_id=1, source_target_pairs={{4,0},{8,4},{12,8},{16,12},{20,16},{24,20},{28,24},{5,1},{9,5},{13... | collective-permute-start | bytes 6152 | tf_op jit(solution)/shard_map/ppermute | solution.py:34
  172.3 5.9 %collective-permute-start.9 = (f32[32,16]{0,1:T(8,128)S(1)}, f32[32,16]{0,1:T(8,128)S(1)}, u32[]{:S(2)}, u32[]{:S(2)}) collective-permute-start(f32[32,16]{0,1:T(8,128)S(1)} %bitcast.116), channel_id=1, source_target_pairs={{0,4},{4,8},{8,12},{12,16},{16,20},{20,24},{24,28},{1,5},{5,9},{9,... | collective-permute-start | bytes 6152 | tf_op jit(solution)/shard_map/ppermute | solution.py:34
where the time goes:
time: 211 us; the launch traced here: 207 us
  other arithmetic  48.2 us (23%)
  blocking collectives  39.6 us (19%)
  local copies, waits for them, and re-layouts  36.5 us (17%)
  waiting for transfers between devices  29.3 us (14%)
  starting transfers between devices  28.6 us (14%)
  matrix products  23.2 us (11%)
    psum x2, blocking collectives, on_device(): gram = lax.psum(jnp.dot(image.T, image, precision=highest), 'sub')  39.6 us
    ppermute x6, waiting for transfers between devices, from_behind(): return lax.ppermute(block, axis, route)  23.6 us
    ppermute x6, starting transfers between devices, from_behind(): return lax.ppermute(block, axis, route)  18.4 us
    reshape x3, local copies, waits for them, and re-layouts, orthonormal(): return solved.reshape(shape_before)  15.5 us
    mul x2, other arithmetic, apply_operator(): ((4.0 + stiff_diag) * vectors - beside + shear_term * others) * inside  12 us
    mul x2, local copies, waits for them, and re-layouts, apply_operator(): ((4.0 + stiff_diag) * vectors - beside + shear_term * others) * inside  8.31 us
    ppermute x2, starting transfers between devices, with_halo(): before = lax.ppermute(last, axis, up)  7.59 us
    another operation x6, other arithmetic, orthonormal(): lower = jnp.linalg.cholesky(gram)  7.19 us
  transfers between devices with their start and end apart: 10, of which 6 were waited for; matrix products, arithmetic and copies ran while one was open for 46% of the time, Pallas kernels for 0%

commit v1 on v0

--- a/solution.py
+++ b/solution.py
@@ -92,7 +92,9 @@
         image = image + jnp.dot(couple_block, rows_next, precision=highest)
         rows_prev = from_behind(own_rows, "sub", 1)
         image = image + jnp.dot(couple_prev.T, rows_prev, precision=highest)
-        gram = lax.psum(jnp.dot(image.T, image, precision=highest), "sub")
+        value = jnp.dot(image.T, image, precision=highest)
+        parts = lax.all_gather(value, "sub")
+        gram = jnp.sum(parts, axis=0)
         lower = jnp.linalg.cholesky(gram)
         own_rows = lax.linalg.triangular_solve(lower, image.T, left_side=True, lower=True).T
     factor = math.sqrt(span_count * 3 * XEXT * YEXT)

time: 211 us -> 233 us (1.10)
  blocking collectives: 39.6 us -> 61.6 us
    all_gather x0 -> x2, blocking collectives: none -> 61.6 us  [on_device(): parts = lax.all_gather(value, 'sub')]
    psum x2 -> x0, blocking collectives: 39.6 us -> none  [on_device(): gram = lax.psum(jnp.dot(image.T, image, precision=highest), 'sub')]
  transfers between devices with their start and end apart: 10 -> 10, of which waited for: 6 -> 6; matrix products, arithmetic and copies ran while one was open for 46% -> 41% of each run, Pallas kernels for 0% -> 0%
where the time goes in v1:
time: 233 us; the launch traced here: 229 us
  blocking collectives  61.6 us (26%)
  other arithmetic  48.3 us (21%)
  local copies, waits for them, and re-layouts  36.5 us (16%)
  waiting for transfers between devices  29.3 us (13%)
  starting transfers between devices  28.6 us (12%)
  matrix products  23.2 us (10%)
    all_gather x2, blocking collectives, on_device(): parts = lax.all_gather(value, 'sub')  61.6 us
    ppermute x6, waiting for transfers between devices, from_behind(): return lax.ppermute(block, axis, route)  23.6 us
    ppermute x6, starting transfers between devices, from_behind(): return lax.ppermute(block, axis, route)  18.4 us
    reshape x3, local copies, waits for them, and re-layouts, orthonormal(): return solved.reshape(shape_before)  15.5 us
    mul x2, other arithmetic, apply_operator(): ((4.0 + stiff_diag) * vectors - beside + shear_term * others) * inside  12 us
    mul x2, local copies, waits for them, and re-layouts, apply_operator(): ((4.0 + stiff_diag) * vectors - beside + shear_term * others) * inside  8.31 us
    ppermute x2, starting transfers between devices, with_halo(): before = lax.ppermute(last, axis, up)  7.59 us
    another operation x6, other arithmetic, orthonormal(): lower = jnp.linalg.cholesky(gram)  7.19 us
  transfers between devices with their start and end apart: 10, of which 6 were waited for; matrix products, arithmetic and copies ran while one was open for 41% of the time, Pallas kernels for 0%

profile of v1, /device:TPU:0, one launch (start us, length us, event | category | flops | bytes accessed | tf_op | source)
XLA Modules:
  0.0 228.8 jit_solution(14026721271305486923)
XLA Ops:
  0.0 4.9 %collective-permute-start.7 = (f32[32,16]{0,1:T(8,128)}, f32[32,16]{0,1:T(8,128)S(1)}, u32[]{:S(2)}, u32[]{:S(2)}) collective-permute-start(f32[32,16]{0,1:T(8,128)} %param.15), channel_id=1, source_target_pairs={{0,4},{4,8},{8,12},{12,16},{16,20},{20,24},{24,28},{1,5},{5,9},{9,... | collective-permute-start | bytes 6152 | tf_op jit(solution)/shard_map/ppermute | solution.py:34
  4.9 1.3 collective-permute-start.5
  6.2 1.2 pad_maximum_fusion.4
  7.4 4.6 %collective-permute-start = (bf16[100,4,128]{2,1,0:T(4,128)(2,1)S(1)}, bf16[100,4,128]{2,1,0:T(4,128)(2,1)S(1)}, u32[]{:S(2)}, u32[]{:S(2)}) collective-permute-start(bf16[100,4,128]{2,1,0:T(4,128)(2,1)S(1)} %get-tuple-element.15), channel_id=1, source_target_pairs={{0,4},{4,8},{8,12},{12,16},{16,20},{20,24},{24,28},{1,5},{5,9},{9,... | collective-permute-start | bytes 307208 | tf_op jit(solution)/shard_map/ppermute | solution.py:25
  11.9 1.3 collective-permute-start.1
  14.2 4.7 %collective-permute-done.1 = bf16[100,4,128]{2,1,0:T(4,128)(2,1)S(1)} collective-permute-done((bf16[100,4,128]{2,1,0:T(4,128)(2,1)S(1)}, bf16[100,4,128]{2,1,0:T(4,128)(2,1)S(1)}, u32[]{:S(2)}, u32[]{:S(2)}) %collective-permute-start.1) | collective-permute-done | bytes 102432 | tf_op jit(solution)/shard_map/ppermute | solution.py:26
  18.9 1.7 pad_maximum_fusion.1
  21.0 0.7 copy.29
  22.4 1.3 collective-permute-start.3
  23.7 3.0 %collective-permute-start.2 = (bf16[100,40,4]{0,1,2:T(8,128)(2,1)S(1)}, bf16[100,40,4]{0,1,2:T(8,128)(2,1)S(1)}, u32[]{:S(2)}, u32[]{:S(2)}) collective-permute-start(bf16[100,40,4]{0,1,2:T(8,128)(2,1)S(1)} %copy.29), channel_id=1, source_target_pairs={{0,1},{1,2},{2,3},{4,5},{5,6},{6,7},{8,9},{9,10},{10,11},{12,13},{... | collective-permute-start | bytes 96008 | tf_op jit(solution)/shard_map/ppermute | solution.py:25
  26.7 0.8 collective-permute-done.2
  28.9 4.9 %pad_maximum_fusion = bf16[100,40,136]{2,1,0:T(8,128)(2,1)S(1)} fusion(bf16[100,40,4]{2,1,0:T(8,128)(2,1)S(1)} %copy.32, bf16[100,4,128]{2,1,0:T(4,128)(2,1)S(1)} %collective-permute-done.1, bf16[1,32,128]{2,1,0:T(8,128)(2,1)S(1)} %bitcast.116, bf16[3,32,128]{2,1,0:T(8,128)(2,1)S(1)} %copy-done.2, bf16[96,32,128]{2,1,0:T(8,128)(2,1)S(1)} %bitcast.107, ...), kind=kLoop, calls=%fused_computation.24 | loop fusion | flops 7616000 | bytes 2176000 | tf_op jit(solution)/shard_map/concatenate | solution.py:27
  35.4 3.0 %add_multiply_fusion.1 = f32[32,3,40,136]{3,0,2,1:T(8,128)S(1)} fusion(f32[32,3,40,136]{3,0,2,1:T(8,128)S(1)} %copy.33, f32[40,136]{1,0:T(8,128)S(1)} %and_convert_fusion, f32[32,40,136]{2,0,1:T(8,128)S(1)} %copy.35, f32[40,136]{1,0:T(8,128)S(1)} %fusion.29, f32[3,40,136]{2,1,0:T(8,128)S(1)} %get-tuple-element.10), kind=kLoop, calls=%fused_computation.20 | loop fusion | flops 4700160 | bytes 4983040 | tf_op jit(solution)/shard_map/mul | solution.py:46
  38.4 3.2 %convolution_bitcast_fusion.2 = f32[32,32]{1,0:T(8,128)S(1)} fusion(f32[32,3,40,136]{3,0,2,1:T(8,128)S(1)} %add_multiply_fusion.1), kind=kOutput, calls=%fused_computation.35 | convolution fusion | flops 200540160 | bytes 2093056 | tf_op jit(solution)/shard_map/dot_general | solution.py:52
  41.6 4.2 %copy.38 = f32[32,3,40,136]{3,2,1,0:T(8,128)} copy(f32[32,3,40,136]{3,0,2,1:T(8,128)S(1)} %add_multiply_fusion.1) | data formatting | bytes 4177920 | tf_op jit(solution)/shard_map/mul | solution.py:46
  45.8 3.6 %reshape.107 = f32[32,16320]{1,0:T(8,128)S(1)} reshape(f32[32,3,40,136]{3,2,1,0:T(8,128)} %copy.38) | data formatting | bytes 4177920 | tf_op jit(solution)/shard_map/reshape | solution.py:51
  49.5 2.9 %cholesky.86 = f32[32,32]{1,0:T(8,128)S(1)} custom-call(f32[32,32]{1,0:T(8,128)S(1)} %fusion.37), custom_call_target="Cholesky" | custom-call | tf_op jit(solution)/shard_map/jit(cholesky)/cholesky | solution.py:53
  53.7 2.4 %custom-call.12 = f32[1,32,32]{1,2,0:T(8,128)S(1)} custom-call(f32[1,32,32]{2,1,0:T(8,128)S(1)} %fusion.30), custom_call_target="InvertDiagBlocksLowerTriangular" | custom-call | tf_op jit(solution)/shard_map/triangular_solve/custom-call.2 | solution.py:54
  56.2 3.3 %fusion.35 = f32[32,16320]{1,0:T(8,128)} fusion(f32[32,16320]{1,0:T(8,128)S(1)} %reshape.107, f32[1,32,32]{1,2,0:T(8,128)S(1)} %custom-call.12), kind=kOutput, calls=%fused_computation.62 | convolution fusion | flops 200540160 | bytes 4182016 | tf_op jit(solution)/shard_map/triangular_solve/dot.1 | solution.py:54
  59.4 5.0 %reshape.108 = f32[32,3,40,136]{3,2,1,0:T(8,128)} reshape(f32[32,16320]{1,0:T(8,128)} %fusion.35) | data formatting | bytes 4177920 | tf_op jit(solution)/shard_map/reshape | solution.py:55
  64.5 5.2 %copy.39 = f32[32,3,40,136]{3,0,2,1:T(8,128)} copy(f32[32,3,40,136]{3,2,1,0:T(8,128)} %reshape.108) | data formatting | bytes 4177920 | tf_op jit(solution)/shard_map/reshape | solution.py:55
  69.7 2.6 %reduce_sum.46 = f32[32,40,136]{2,1,0:T(8,128)S(1)} reduce(f32[32,3,40,136]{3,2,1,0:T(8,128)} %reshape.108, f32[]{:T(128)} %constant.80.clone.1), dimensions={1}, to_apply=%region_3.0 | reduce | flops 348160 | bytes 2785284 | tf_op jit(solution)/shard_map/reduce_sum | solution.py:45
  72.7 9.0 %add_multiply_fusion = f32[32,3,40,136]{3,0,2,1:T(8,128)S(1)} fusion(f32[32,3,40,136]{3,0,2,1:T(8,128)} %copy.39, f32[32,40,136]{2,0,1:T(8,128)S(1)} %copy.41, f32[40,136]{1,0:T(8,128)S(1)} %and_convert_fusion, f32[40,136]{1,0:T(8,128)S(1)} %fusion.29, f32[3,40,136]{2,1,0:T(8,128)S(1)} %get-tuple-element.10), kind=kLoop, calls=%fused_computation.16 | loop fusion | flops 4700160 | bytes 4983040 | tf_op jit(solution)/shard_map/mul | solution.py:46
  81.7 3.2 %convolution_bitcast_fusion.1 = f32[32,32]{1,0:T(8,128)S(1)} fusion(f32[32,3,40,136]{3,0,2,1:T(8,128)S(1)} %add_multiply_fusion), kind=kOutput, calls=%fused_computation.34 | convolution fusion | flops 200540160 | bytes 2093056 | tf_op jit(solution)/shard_map/dot_general | solution.py:52
  84.9 4.2 %copy.44 = f32[32,3,40,136]{3,2,1,0:T(8,128)} copy(f32[32,3,40,136]{3,0,2,1:T(8,128)S(1)} %add_multiply_fusion) | data formatting | bytes 4177920 | tf_op jit(solution)/shard_map/mul | solution.py:46
  89.0 3.1 %reshape.109 = f32[32,16320]{1,0:T(8,128)S(1)} reshape(f32[32,3,40,136]{3,2,1,0:T(8,128)} %copy.44) | data formatting | bytes 4177920 | tf_op jit(solution)/shard_map/reshape | solution.py:51
  92.2 2.9 %cholesky.97 = f32[32,32]{1,0:T(8,128)S(1)} custom-call(f32[32,32]{1,0:T(8,128)S(1)} %fusion.34), custom_call_target="Cholesky" | custom-call | tf_op jit(solution)/shard_map/jit(cholesky)/cholesky | solution.py:53
  96.5 2.4 %custom-call.13 = f32[1,32,32]{1,2,0:T(8,128)S(1)} custom-call(f32[1,32,32]{2,1,0:T(8,128)S(1)} %fusion.31), custom_call_target="InvertDiagBlocksLowerTriangular" | custom-call | tf_op jit(solution)/shard_map/triangular_solve/custom-call.2 | solution.py:54
  98.9 3.3 %fusion.32 = f32[32,16320]{1,0:T(8,128)} fusion(f32[32,16320]{1,0:T(8,128)S(1)} %reshape.109, f32[1,32,32]{1,2,0:T(8,128)S(1)} %custom-call.13), kind=kOutput, calls=%fused_computation.58 | convolution fusion | flops 200540160 | bytes 4182016 | tf_op jit(solution)/shard_map/triangular_solve/dot.1 | solution.py:54
  102.2 5.2 %reshape.110 = f32[32,3,40,136]{3,2,1,0:T(8,128)} reshape(f32[32,16320]{1,0:T(8,128)} %fusion.32) | data formatting | bytes 4177920 | tf_op jit(solution)/shard_map/reshape | solution.py:55
  107.4 3.9 %fusion.52 = (f32[32,40,136]{2,0,1:T(8,128)S(1)}, f32[32,3,40,136]{3,0,2,1:T(8,128)S(1)}) fusion(f32[32]{0:T(128)S(1)} %compare_convert_fusion, f32[32,3,40,136]{3,2,1,0:T(8,128)} %reshape.110), kind=kLoop, calls=%fused_computation.97 | loop fusion | flops 870400 | bytes 4874368 | tf_op jit(solution)/shard_map/reduce_sum | solution.py:45
  111.4 5.0 %fusion.25 = f32[32,32]{1,0:T(8,128)S(1)} fusion(f32[32,3,40,136]{3,0,2,1:T(8,128)S(1)} %get-tuple-element.8, f32[32,40,136]{2,0,1:T(8,128)S(1)} %get-tuple-element.6, f32[40,136]{1,0:T(8,128)S(1)} %and_convert_fusion, f32[40,136]{1,0:T(8,128)S(1)} %fusion.29, f32[3,40,136]{2,1,0:T(8,128)S(1)} %get-tuple-element.10), kind=kOutput, calls=%fused_computation.33 | convolution fusion | flops 205240320 | bytes 9383936 | tf_op jit(solution)/shard_map/dot_general | solution.py:64
  116.4 1.3 collective-permute-start.4
  117.9 21.1 %collective-permute-done.4 = f32[32,3,8,136]{3,0,2,1:T(8,128)S(1)} collective-permute-done((f32[32,3,8,136]{3,0,2,1:T(8,128)S(1)}, f32[32,3,8,136]{3,0,2,1:T(8,128)S(1)}, u32[]{:S(2)}, u32[]{:S(2)}) %collective-permute-start.4) | collective-permute-done | bytes 417824 | tf_op jit(solution)/shard_map/ppermute | solution.py:34
  139.0 0.8 convolution_bitcast_fusion
  139.8 5.1 %collective-permute-start.6 = (f32[32,32]{1,0:T(8,128)S(1)}, f32[32,32]{1,0:T(8,128)S(1)}, u32[]{:S(2)}, u32[]{:S(2)}) collective-permute-start(f32[32,32]{1,0:T(8,128)S(1)} %convolution_bitcast_fusion), channel_id=1, source_target_pairs={{0,4},{4,8},{8,12},{12,16},{16,20},{20,24},{24,28},{1,5},{5,9},{9,... | collective-permute-start | bytes 12296 | tf_op jit(solution)/shard_map/ppermute | solution.py:34
  145.0 1.3 collective-permute-done.6
  146.6 31.0 %all-gather = f32[128,16]{1,0:T(8,128)S(1)} all-gather(f32[16,16]{1,0:T(8,128)S(1)} %fusion.55), channel_id=2, replica_groups=mesh['sub'=8,'sec'=4] {'sub'}, dimensions={0}, use_global_device_ids=true | all-gather | bytes 9216 | tf_op jit(solution)/shard_map/all_gather | solution.py:96
  177.7 1.5 cholesky.108
  180.5 1.2 custom-call.14
  181.9 1.3 collective-permute-start.8
  183.4 4.6 %collective-permute-start.9 = (f32[32,16]{0,1:T(8,128)S(1)}, f32[32,16]{0,1:T(8,128)S(1)}, u32[]{:S(2)}, u32[]{:S(2)}) collective-permute-start(f32[32,16]{0,1:T(8,128)S(1)} %bitcast.120), channel_id=1, source_target_pairs={{0,4},{4,8},{8,12},{12,16},{16,20},{20,24},{24,28},{1,5},{5,9},{9,... | collective-permute-start | bytes 6152 | tf_op jit(solution)/shard_map/ppermute | solution.py:34
  188.1 1.2 collective-permute-done.9
  189.5 30.5 %all-gather.1 = f32[128,16]{1,0:T(8,128)S(1)} all-gather(f32[16,16]{1,0:T(8,128)S(1)} %fusion.57), channel_id=3, replica_groups=mesh['sub'=8,'sec'=4] {'sub'}, dimensions={0}, use_global_device_ids=true | all-gather | bytes 9216 | tf_op jit(solution)/shard_map/all_gather | solution.py:96
  220.2 1.5 cholesky.119
  223.0 1.2 custom-call.15
  224.4 3.0 %fusion.22 = f32[16,3,32,128]{3,0,2,1:T(8,128)S(1)} fusion(f32[16,32,1,1]{1,0,3,2:T(8,128)S(1)} %convolution_bitcast_fusion.3, f32[32,3,40,136]{3,0,2,1:T(8,128)} %copy-done.1), kind=kOutput, calls=%fused_computation.31 | convolution fusion | flops 75694080 | bytes 2361344 | tf_op jit(solution)/shard_map/ak,acxy->kcxy/dot_general | solution.py:102
  227.5 1.1 copy.48
  (64 shorter events, 11.9 us)
Async XLA Ops:
  0.0 145.0 %collective-permute-start.7 = (f32[32,16]{0,1:T(8,128)}, f32[32,16]{0,1:T(8,128)S(1)}, u32[]{:S(2)}, u32[]{:S(2)}) collective-permute-start(f32[32,16]{0,1:T(8,128)} %param.15), channel_id=1, source_target_pairs={{0,4},{4,8},{8,12},{12,16},{16,20},{20,24},{24,28},{1,5},{5,9},{9,... | collective-permute-start | bytes 6152 | tf_op jit(solution)/shard_map/ppermute | solution.py:34
  4.9 140.0 %collective-permute-start.5 = (f32[32,16]{0,1:T(8,128)}, f32[32,16]{0,1:T(8,128)S(1)}, u32[]{:S(2)}, u32[]{:S(2)}) collective-permute-start(f32[32,16]{0,1:T(8,128)} %param.15), channel_id=1, source_target_pairs={{4,0},{8,4},{12,8},{16,12},{20,16},{24,20},{28,24},{5,1},{9,5},{13... | collective-permute-start | bytes 6152 | tf_op jit(solution)/shard_map/ppermute | solution.py:34
  7.4 6.8 %collective-permute-start = (bf16[100,4,128]{2,1,0:T(4,128)(2,1)S(1)}, bf16[100,4,128]{2,1,0:T(4,128)(2,1)S(1)}, u32[]{:S(2)}, u32[]{:S(2)}) collective-permute-start(bf16[100,4,128]{2,1,0:T(4,128)(2,1)S(1)} %get-tuple-element.15), channel_id=1, source_target_pairs={{0,4},{4,8},{8,12},{12,16},{16,20},{20,24},{24,28},{1,5},{5,9},{9,... | collective-permute-start | bytes 307208 | tf_op jit(solution)/shard_map/ppermute | solution.py:25
  11.9 7.0 %collective-permute-start.1 = (bf16[100,4,128]{2,1,0:T(4,128)(2,1)S(1)}, bf16[100,4,128]{2,1,0:T(4,128)(2,1)S(1)}, u32[]{:S(2)}, u32[]{:S(2)}) collective-permute-start(bf16[100,4,128]{2,1,0:T(4,128)(2,1)S(1)} %get-tuple-element.16), channel_id=1, source_target_pairs={{4,0},{8,4},{12,8},{16,12},{20,16},{24,20},{28,24},{5,1},{9,5},{13... | collective-permute-start | bytes 307208 | tf_op jit(solution)/shard_map/ppermute | solution.py:26
  20.6 8.2 %copy-start = (bf16[32,3,32,128]{3,2,1,0:T(8,128)(2,1)S(1)}, bf16[32,3,32,128]{3,2,1,0:T(8,128)(2,1)}, u32[]{:S(2)}) copy-start(bf16[32,3,32,128]{3,2,1,0:T(8,128)(2,1)} %param.11) | copy-start | bytes 2359300
  20.6 8.2 %copy-start.2 = (bf16[3,32,128]{2,1,0:T(8,128)(2,1)S(1)}, bf16[3,32,128]{2,1,0:T(8,128)(2,1)}, u32[]{:S(2)}) copy-start(bf16[3,32,128]{2,1,0:T(8,128)(2,1)} %param.12) | copy-start | bytes 73732
  20.6 8.2 %copy-start.3 = (bf16[32,128]{1,0:T(8,128)(2,1)S(1)}, bf16[32,128]{1,0:T(8,128)(2,1)}, u32[]{:S(2)}) copy-start(bf16[32,128]{1,0:T(8,128)(2,1)} %param.13) | copy-start | bytes 24580
  22.4 5.8 %collective-permute-start.3 = (bf16[100,40,4]{0,1,2:T(8,128)(2,1)S(1)}, bf16[100,40,4]{0,1,2:T(8,128)(2,1)S(1)}, u32[]{:S(2)}, u32[]{:S(2)}) collective-permute-start(bf16[100,40,4]{0,1,2:T(8,128)(2,1)S(1)} %copy.30), channel_id=1, source_target_pairs={{1,0},{2,1},{3,2},{5,4},{6,5},{7,6},{9,8},{10,9},{11,10},{13,12},{... | collective-permute-start | bytes 96008 | tf_op jit(solution)/shard_map/ppermute | solution.py:26
  23.7 3.9 %collective-permute-start.2 = (bf16[100,40,4]{0,1,2:T(8,128)(2,1)S(1)}, bf16[100,40,4]{0,1,2:T(8,128)(2,1)S(1)}, u32[]{:S(2)}, u32[]{:S(2)}) collective-permute-start(bf16[100,40,4]{0,1,2:T(8,128)(2,1)S(1)} %copy.29), channel_id=1, source_target_pairs={{0,1},{1,2},{2,3},{4,5},{5,6},{6,7},{8,9},{9,10},{10,11},{12,13},{... | collective-permute-start | bytes 96008 | tf_op jit(solution)/shard_map/ppermute | solution.py:25
  111.3 27.6 %copy-start.1 = (f32[32,3,40,136]{3,0,2,1:T(8,128)}, f32[32,3,40,136]{3,0,2,1:T(8,128)S(1)}, u32[]{:S(2)}) copy-start(f32[32,3,40,136]{3,0,2,1:T(8,128)S(1)} %get-tuple-element.8) | copy-start | bytes 6266884
  111.4 6.3 %copy-start.4 = (f32[32,16]{0,1:T(8,128)S(1)}, f32[32,16]{0,1:T(8,128)}, u32[]{:S(2)}) copy-start(f32[32,16]{0,1:T(8,128)} %param.15) | copy-start | bytes 6148
  116.4 22.6 %collective-permute-start.4 = (f32[32,3,8,136]{3,0,2,1:T(8,128)S(1)}, f32[32,3,8,136]{3,0,2,1:T(8,128)S(1)}, u32[]{:S(2)}, u32[]{:S(2)}) collective-permute-start(f32[32,3,8,136]{3,0,2,1:T(8,128)S(1)} %slice.109), channel_id=1, source_target_pairs={{4,0},{8,4},{12,8},{16,12},{20,16},{24,20},{28,24},{5,1},{9,5},{13... | collective-permute-start | bytes 1253384 | tf_op jit(solution)/shard_map/ppermute | solution.py:34
  139.8 6.5 %collective-permute-start.6 = (f32[32,32]{1,0:T(8,128)S(1)}, f32[32,32]{1,0:T(8,128)S(1)}, u32[]{:S(2)}, u32[]{:S(2)}) collective-permute-start(f32[32,32]{1,0:T(8,128)S(1)} %convolution_bitcast_fusion), channel_id=1, source_target_pairs={{0,4},{4,8},{8,12},{12,16},{16,20},{20,24},{24,28},{1,5},{5,9},{9,... | collective-permute-start | bytes 12296 | tf_op jit(solution)/shard_map/ppermute | solution.py:34
  181.9 6.0 %collective-permute-start.8 = (f32[32,16]{0,1:T(8,128)S(1)}, f32[32,16]{0,1:T(8,128)S(1)}, u32[]{:S(2)}, u32[]{:S(2)}) collective-permute-start(f32[32,16]{0,1:T(8,128)S(1)} %bitcast.119), channel_id=1, source_target_pairs={{4,0},{8,4},{12,8},{16,12},{20,16},{24,20},{28,24},{5,1},{9,5},{13... | collective-permute-start | bytes 6152 | tf_op jit(solution)/shard_map/ppermute | solution.py:34
  183.4 5.9 %collective-permute-start.9 = (f32[32,16]{0,1:T(8,128)S(1)}, f32[32,16]{0,1:T(8,128)S(1)}, u32[]{:S(2)}, u32[]{:S(2)}) collective-permute-start(f32[32,16]{0,1:T(8,128)S(1)} %bitcast.120), channel_id=1, source_target_pairs={{0,4},{4,8},{8,12},{12,16},{16,20},{20,24},{24,28},{1,5},{5,9},{9,... | collective-permute-start | bytes 6152 | tf_op jit(solution)/shard_map/ppermute | solution.py:34
